TPU v7x, 512 devices: a whole 4x8x8 slice. The times are simulated.
512 devices in a mesh: src: 4 (over x_hi, core), depth: 8 (over y), lat: 16 (over z, x_lo).
Axes of the slice: x: 4 (x_hi: 2, x_lo: 2; x = x_hi * 2 + x_lo), y: 8, z: 8, core: 2. Of those that a mesh axis runs over, the one named last changes fastest.
Arguments:
- conductivity: float32 [128, 128, 128], P('depth', 'lat'), may hold values from 0.2 to 2
- e_start: float32 [8, 3, 128, 128, 128], P('src', None, 'depth', 'lat'), may hold values from -6 to 6
- h_start: float32 [8, 3, 128, 128, 128], P('src', None, 'depth', 'lat'), may hold values from -6 to 6
- e_weight: float32 [8, 3, 128, 128, 128], P('src', None, 'depth', 'lat'), may hold values from -6 to 6
- h_weight: float32 [8, 3, 128, 128, 128], P('src', None, 'depth', 'lat'), may hold values from -6 to 6
- source_amp: float32 [8, 3], P('src'), may hold values from -12 to 12
- tow_cell: int32 [8], P('src'), may hold values from 0 to 2097151
- rec_cell: int32 [8, 16, 16], P('depth', 'lat'), may hold values from 0 to 16383
- rec_owner: int32 [8, 16, 16, 1], P('depth', 'lat'), may hold values from 0 to 15; in each aligned block of 16 rows (0 to 15, 16 to 31, ..., all dimensions but the last counted through in order) at most 2 rows name the same one
Outputs:
- grad: float32 [128, 128, 128], P('depth', 'lat')
- line_samples: float32 [8, 8, 16, 16, 2, 9], P('src', 'depth', 'lat')
Inputs may be any that keep to these rules, and one draw needn't show every extreme that they name: `tow_cell`: a flat cell of the whole grid. `rec_cell`: a local flat cell of the receiver's block; cells may repeat. `rec_owner`: among the 16 receivers of one block, at most 2 have the same owner, and in some block exactly 2 do.
All inputs are finite; a program needn't handle non-finite values.
Results may differ from a plain program's by a relative error of at most 0.0003.
Values sent between devices are 32-bit elements; how exact they have to be, the bound alone decides.
No kernel may reach another device: no remote copies, remote signals or barrier semaphores. Data moves between devices by JAX's collectives and lax.ppermute only.
A program may use at most 128 MiB of HBM per device.

v0:
```python
import jax
import jax.numpy as jnp
from jax import lax
from jax.sharding import PartitionSpec as P

ch_coef = 0.5
loss_rate = 0.5


def passed_along(block, axis, distance):
    devices = range(lax.axis_size(axis))
    route = [(i - distance, i) for i in devices if i - distance in devices]
    return lax.ppermute(block, axis, route)


def component(field, k):
    return field[..., k, :, :, :]


def curl_upper(field, rim_z, rim_x):
    fx = component(field, 0)
    fy = component(field, 1)
    fz = component(field, 2)
    zx = jnp.concatenate([fx, component(rim_z, 0)], axis=-3)[..., 1:, :, :] - fx
    zy = jnp.concatenate([fy, component(rim_z, 1)], axis=-3)[..., 1:, :, :] - fy
    xy = jnp.concatenate([fy, component(rim_x, 0)], axis=-2)[..., :, 1:, :] - fy
    xz = jnp.concatenate([fz, component(rim_x, 1)], axis=-2)[..., :, 1:, :] - fz
    yz = jnp.concatenate([fz[..., 1:], jnp.zeros_like(fz[..., :1])], axis=-1) - fz
    yx = jnp.concatenate([fx[..., 1:], jnp.zeros_like(fx[..., :1])], axis=-1) - fx
    return jnp.stack([yz - zy, zx - xz, xy - yx], axis=-4)


def curl_lower(field, rim_z, rim_x):
    fx = component(field, 0)
    fy = component(field, 1)
    fz = component(field, 2)
    zx = fx - jnp.concatenate([component(rim_z, 0), fx], axis=-3)[..., :-1, :, :]
    zy = fy - jnp.concatenate([component(rim_z, 1), fy], axis=-3)[..., :-1, :, :]
    xy = fy - jnp.concatenate([component(rim_x, 0), fy], axis=-2)[..., :, :-1, :]
    xz = fz - jnp.concatenate([component(rim_x, 1), fz], axis=-2)[..., :, :-1, :]
    yz = fz - jnp.concatenate([jnp.zeros_like(fz[..., :1]), fz[..., :-1]], axis=-1)
    yx = fx - jnp.concatenate([jnp.zeros_like(fx[..., :1]), fx[..., :-1]], axis=-1)
    return jnp.stack([yz - zy, zx - xz, xy - yx], axis=-4)


def coefficients(sigma):
    denom = 1.0 + loss_rate * sigma
    decay = (1.0 - loss_rate * sigma) / denom
    gain = ch_coef / denom
    decay_slope = -2.0 * loss_rate / (denom * denom)
    gain_slope = -ch_coef * loss_rate / (denom * denom)
    return (decay, gain, decay_slope, gain_slope)


def upper_rims(field):
    rim_z = passed_along(field[:, 0:2, 0:1], "depth", -1)
    rim_x = passed_along(field[:, 1:3, :, 0:1], "lat", -1)
    return (rim_z, rim_x)


def lower_rims(field):
    rim_z = passed_along(field[:, 0:2, -1:], "depth", 1)
    rim_x = passed_along(field[:, 1:3, :, -1:], "lat", 1)
    return (rim_z, rim_x)


def leap_one(first, second, scale):
    scaled = scale * first
    rim_z, rim_x = upper_rims(scaled)
    updated = second + curl_upper(scaled, rim_z, rim_x)
    low_z, low_x = lower_rims(updated)
    return (updated, curl_lower(updated, low_z, low_x))


def per_device(
    conductivity, e_start, h_start, e_weight, h_weight, source_amp, tow_cell, rec_cell, rec_owner
):
    groups, _, depth_cells, lat_cells, width = e_start.shape
    steps_total = source_amp.shape[1]
    tiles = lax.axis_size("lat")
    capacity = max(2, rec_cell.shape[-1] // tiles)
    depth_at = lax.axis_index("depth")
    lat_at = lax.axis_index("lat")
    decay, gain, decay_slope, gain_slope = coefficients(conductivity)
    margin = 0
    decay_use, gain_use = (decay, gain)
    e_field, h_field, lam_e, lam_h = (e_start, h_start, e_weight, h_weight)

    def leap(first, second, scale):
        return leap_one(first, second, scale)

    plane = lat_cells * tiles * width
    local_z = tow_cell // plane - depth_at * depth_cells + margin
    local_x = tow_cell // width % (lat_cells * tiles) - lat_at * lat_cells + margin
    local_y = tow_cell % width
    grid_z = jnp.arange(depth_cells + 2 * margin)[:, None, None]
    grid_x = jnp.arange(lat_cells + 2 * margin)[None, :, None]
    grid_y = jnp.arange(width)[None, None, :]
    point = (
        (grid_z[None] == local_z[:, None, None, None])
        & (grid_x[None] == local_x[:, None, None, None])
        & (grid_y[None] == local_y[:, None, None, None])
    ).astype(jnp.float32)
    blank = jnp.zeros_like(point)
    owner = rec_owner.reshape(-1)
    cells = rec_cell.reshape(-1)
    order = jnp.arange(owner.shape[0])
    rank = jnp.sum(
        ((owner[:, None] == owner[None, :]) & (order[None, :] < order[:, None])).astype(jnp.int32),
        axis=1,
    )
    hot = (
        (owner[:, None, None] == jnp.arange(tiles)[:, None])
        & (rank[:, None, None] == jnp.arange(capacity)[None, :])
    ).astype(jnp.float32)
    kept = []
    delivered = []
    for step in range(steps_total):
        h_field, turned = leap(e_field, h_field, -ch_coef)
        source = source_amp[:, step][:, None, None, None] * point
        drive = turned - jnp.stack([source, blank, blank], axis=1)
        kept.append((e_field, drive))
        e_field = decay_use * e_field + gain_use * drive
        sampled = jnp.take(e_field.reshape(groups, 3, -1), cells, axis=2)
        placed = jnp.sum(sampled[:, :, :, None, None] * hot[None, None], axis=2)
        delivered.append(
            lax.all_to_all(
                jnp.transpose(placed, (0, 2, 3, 1)), "lat", split_axis=1, concat_axis=1, tiled=True
            )
        )
    received = jnp.concatenate(delivered, axis=-1)
    line_samples = received.reshape(groups, 1, 1, tiles, capacity, 3 * steps_total)
    local = jnp.zeros((depth_cells, lat_cells, width), jnp.float32)
    for step in range(steps_total - 1, -1, -1):
        e_old, drive = kept[step]
        weight_now = lam_e
        term = jnp.sum(
            decay_slope * e_old * weight_now + gain_slope * drive * weight_now, axis=(0, 1)
        )
        local = local + term
        if step > 0:
            lam_h, turned = leap(lam_e, lam_h, gain)
            lam_e = decay_use * lam_e - ch_coef * turned
    total = lax.psum(local, "src")
    return (total, line_samples)


def solution(mesh):
    placed = (
        P("depth", "lat", None),
        P("src", None, "depth", "lat", None),
        P("src", None, "depth", "lat", None),
        P("src", None, "depth", "lat", None),
        P("src", None, "depth", "lat", None),
        P("src", None),
        P("src"),
        P("depth", "lat", None),
        P("depth", "lat", None, None),
    )
    return jax.shard_map(
        per_device,
        mesh=mesh,
        in_specs=placed,
        out_specs=(P("depth", "lat", None), P("src", "depth", "lat", None, None, None)),
        check_vma=False,
    )
```

profile of v0, /device:TPU:1, one launch (start us, length us, event | category | flops | bytes accessed | tf_op | source)
XLA Modules:
  0.0 280.9 jit_solution(6807090759365684788)
XLA Ops:
  8.3 1.3 collective-permute-start
  9.6 1.3 collective-permute-start.1
  13.2 1.2 compare_and_fusion
  16.4 1.5 multiply_divide_fusion.1
  19.2 1.1 maximum_add_fusion
  20.3 4.7 %collective-permute-start.2 = (f32[2,2,1,8,128]{4,0,3,2,1:T(2,128)S(1)}, f32[2,2,1,8,128]{4,0,3,2,1:T(2,128)S(1)}, u32[]{:S(2)}, u32[]{:S(2)}) collective-permute-start(f32[2,2,1,8,128]{4,0,3,2,1:T(2,128)S(1)} %bitcast.362), channel_id=1, source_target_pairs={{0,16},{16,32},{32,48},{48,64},{64,80},{80,96},{96,112},{1,17},{17... | collective-permute-start | bytes 49160 | tf_op jit(solution)/shard_map/ppermute | solution.py:13
  25.0 4.0 %collective-permute-start.3 = (f32[2,2,16,1,128]{4,2,0,3,1:T(8,128)S(1)}, f32[2,2,16,1,128]{4,2,0,3,1:T(8,128)S(1)}, u32[]{:S(2)}, u32[]{:S(2)}) collective-permute-start(f32[2,2,16,1,128]{4,2,0,3,1:T(8,128)S(1)} %slice.636), channel_id=1, source_target_pairs={{0,1},{1,2},{2,3},{3,4},{4,5},{5,6},{6,7},{7,8},{8,9},{9,10},{10,1... | collective-permute-start | bytes 98312 | tf_op jit(solution)/shard_map/ppermute | solution.py:13
  30.3 1.2 multiply_add_fusion.2
  31.6 1.3 collective-permute-start.4
  33.0 11.4 %copy.327 = f32[2,3,16,8,128]{1,0,4,3,2:T(2,128)} copy(f32[2,3,16,8,128]{4,3,2,0,1:T(8,128)S(1)} %multiply_add_fusion.2) | data formatting | bytes 786432 | tf_op jit(solution)/shard_map/add | solution.py:123
  44.5 1.3 collective-permute-start.5
  46.0 6.9 %gather_fusion = f32[16,2,3]{2,1,0:T(2,128)} fusion(f32[2,3,16384]{1,0,2:T(2,128)} %bitcast.334, s32[1024]{0:T(1024)S(1)} %pad_clamp_fusion), kind=kCustom, calls=%fused_computation.clone | custom fusion | bytes 832 | tf_op jit(solution)/shard_map/jit(_take)/gather | solution.py:124
  53.7 4.0 %collective-permute-start.6 = (f32[2,2,1,8,128]{4,3,0,2,1:T(8,128)S(1)}, f32[2,2,1,8,128]{4,3,0,2,1:T(8,128)S(1)}, u32[]{:S(2)}, u32[]{:S(2)}) collective-permute-start(f32[2,2,1,8,128]{4,3,0,2,1:T(8,128)S(1)} %slice_bitcast_fusion.44), channel_id=1, source_target_pairs={{0,16},{16,32},{32,48},{48,64},{64,80},{80,96},{96,112},{1,17},{17... | collective-permute-start | bytes 49160 | tf_op jit(solution)/shard_map/ppermute | solution.py:13
  57.7 4.8 %collective-permute-start.7 = (f32[2,2,16,1,128]{4,3,2,0,1:T(1,128)S(1)}, f32[2,2,16,1,128]{4,3,2,0,1:T(1,128)S(1)}, u32[]{:S(2)}, u32[]{:S(2)}) collective-permute-start(f32[2,2,16,1,128]{4,3,2,0,1:T(1,128)S(1)} %slice.658), channel_id=1, source_target_pairs={{0,1},{1,2},{2,3},{3,4},{4,5},{5,6},{6,7},{7,8},{8,9},{9,10},{10,1... | collective-permute-start | bytes 98312 | tf_op jit(solution)/shard_map/ppermute | solution.py:13
  65.3 1.3 collective-permute-start.8
  70.6 1.3 collective-permute-start.9
  71.9 1.3 collective-permute-start.12
  74.7 1.3 collective-permute-start.13
  76.0 11.4 %copy.330 = f32[2,3,16,8,128]{1,0,4,3,2:T(2,128)} copy(f32[2,3,16,8,128]{4,3,2,0,1:T(8,128)S(1)} %get-tuple-element.18) | data formatting | bytes 786432 | tf_op jit(solution)/shard_map/add | solution.py:123
  87.4 7.1 %gather_fusion.1 = f32[16,2,3]{2,1,0:T(2,128)} fusion(f32[2,3,16384]{1,0,2:T(2,128)} %bitcast.336, s32[1024]{0:T(1024)} %copy-done.18), kind=kCustom, calls=%fused_computation.1.clone | custom fusion | bytes 832 | tf_op jit(solution)/shard_map/jit(_take)/gather | solution.py:124
  96.7 1.1 fusion.59
  97.8 1.2 fusion.63
  99.1 1.2 maximum_add_fusion.2
  100.4 4.6 %collective-permute-start.10 = (f32[2,2,1,8,128]{4,3,0,2,1:T(8,128)S(1)}, f32[2,2,1,8,128]{4,3,0,2,1:T(8,128)S(1)}, u32[]{:S(2)}, u32[]{:S(2)}) collective-permute-start(f32[2,2,1,8,128]{4,3,0,2,1:T(8,128)S(1)} %slice_bitcast_fusion.38), channel_id=1, source_target_pairs={{0,16},{16,32},{32,48},{48,64},{64,80},{80,96},{96,112},{1,17},{17... | collective-permute-start | bytes 49160 | tf_op jit(solution)/shard_map/ppermute | solution.py:13
  105.7 1.1 fusion.39
  106.9 1.3 fusion.43
  109.3 5.8 %collective-permute-start.11 = (f32[2,2,16,1,128]{4,3,2,0,1:T(1,128)S(1)}, f32[2,2,16,1,128]{4,3,2,0,1:T(1,128)S(1)}, u32[]{:S(2)}, u32[]{:S(2)}) collective-permute-start(f32[2,2,16,1,128]{4,3,2,0,1:T(1,128)S(1)} %slice.680), channel_id=1, source_target_pairs={{0,1},{1,2},{2,3},{3,4},{4,5},{5,6},{6,7},{7,8},{8,9},{9,10},{10,1... | collective-permute-start | bytes 98312 | tf_op jit(solution)/shard_map/ppermute | solution.py:13
  115.2 4.1 %collective-permute-start.14 = (f32[2,2,1,8,128]{4,3,0,2,1:T(8,128)S(1)}, f32[2,2,1,8,128]{4,3,0,2,1:T(8,128)S(1)}, u32[]{:S(2)}, u32[]{:S(2)}) collective-permute-start(f32[2,2,1,8,128]{4,3,0,2,1:T(8,128)S(1)} %copy.349), channel_id=1, source_target_pairs={{0,16},{16,32},{32,48},{48,64},{64,80},{80,96},{96,112},{1,17},{17... | collective-permute-start | bytes 49160 | tf_op jit(solution)/shard_map/ppermute | solution.py:13
  119.3 4.5 %collective-permute-start.15 = (f32[2,2,16,1,128]{4,2,0,3,1:T(8,128)S(1)}, f32[2,2,16,1,128]{4,2,0,3,1:T(8,128)S(1)}, u32[]{:S(2)}, u32[]{:S(2)}) collective-permute-start(f32[2,2,16,1,128]{4,2,0,3,1:T(8,128)S(1)} %copy.351), channel_id=1, source_target_pairs={{0,1},{1,2},{2,3},{3,4},{4,5},{5,6},{6,7},{7,8},{8,9},{9,10},{10,1... | collective-permute-start | bytes 98312 | tf_op jit(solution)/shard_map/ppermute | solution.py:13
  125.2 2.5 multiply_add_fusion
  127.7 12.7 %copy.333 = f32[2,3,16,8,128]{1,0,4,3,2:T(2,128)} copy(f32[2,3,16,8,128]{4,3,2,0,1:T(8,128)} %get-tuple-element.21) | data formatting | bytes 786432 | tf_op jit(solution)/shard_map/add | solution.py:123
  140.4 6.5 %gather_fusion.2 = f32[16,2,3]{2,1,0:T(2,128)S(1)} fusion(f32[2,3,16384]{1,0,2:T(2,128)} %bitcast.335, s32[1024]{0:T(1024)} %copy-done.18), kind=kCustom, calls=%fused_computation.2.clone | custom fusion | bytes 832 | tf_op jit(solution)/shard_map/jit(_take)/gather | solution.py:124
  148.2 14.6 %all-to-all-start.2 = ((f32[2,16,2,3]{3,2,0,1:T(2,128)}), f32[2,16,2,3]{3,2,0,1:T(2,128)S(1)}, u32[]{:S(2)}, u32[]{:S(2)}) async-start(f32[2,16,2,3]{3,2,0,1:T(2,128)} %copy.335), calls=%async_computation.2 | async-start | bytes 65536 | tf_op jit(solution)/shard_map/all_to_all | solution.py:127
  163.4 6.9 %all-to-all-done.2 = f32[2,16,2,3]{3,2,0,1:T(2,128)S(1)} async-done(((f32[2,16,2,3]{3,2,0,1:T(2,128)}), f32[2,16,2,3]{3,2,0,1:T(2,128)S(1)}, u32[]{:S(2)}, u32[]{:S(2)}) %all-to-all-start.2) | async-done | bytes 800 | tf_op jit(solution)/shard_map/all_to_all | solution.py:127
  170.3 3.5 %all-to-all-start.1 = ((f32[2,16,2,3]{3,2,0,1:T(2,128)}), f32[2,16,2,3]{3,2,0,1:T(2,128)S(1)}, u32[]{:S(2)}, u32[]{:S(2)}) async-start(f32[2,16,2,3]{3,2,0,1:T(2,128)} %copy.332), calls=%async_computation.1 | async-start | bytes 65536 | tf_op jit(solution)/shard_map/all_to_all | solution.py:127
  174.4 1.3 collective-permute-start.16
  176.4 5.0 %all-to-all-done.1 = f32[2,16,2,3]{3,2,0,1:T(2,128)S(1)} async-done(((f32[2,16,2,3]{3,2,0,1:T(2,128)}), f32[2,16,2,3]{3,2,0,1:T(2,128)S(1)}, u32[]{:S(2)}, u32[]{:S(2)}) %all-to-all-start.1) | async-done | bytes 800 | tf_op jit(solution)/shard_map/all_to_all | solution.py:127
  181.4 4.1 %all-to-all-start = ((f32[2,16,2,3]{3,2,0,1:T(2,128)}), f32[2,16,2,3]{3,2,0,1:T(2,128)}, u32[]{:S(2)}, u32[]{:S(2)}) async-start(f32[2,16,2,3]{3,2,0,1:T(2,128)} %copy.329), calls=%async_computation | async-start | bytes 65536 | tf_op jit(solution)/shard_map/all_to_all | solution.py:127
  187.1 1.3 collective-permute-start.17
  190.1 3.0 %all-to-all-done = f32[2,16,2,3]{3,2,0,1:T(2,128)} async-done(((f32[2,16,2,3]{3,2,0,1:T(2,128)}), f32[2,16,2,3]{3,2,0,1:T(2,128)}, u32[]{:S(2)}, u32[]{:S(2)}) %all-to-all-start) | async-done | bytes 800 | tf_op jit(solution)/shard_map/all_to_all | solution.py:127
  193.1 1.4 copy.336
  196.1 1.1 fusion.23
  197.3 4.6 %collective-permute-start.18 = (f32[2,2,1,8,128]{4,3,0,2,1:T(8,128)S(1)}, f32[2,2,1,8,128]{4,3,0,2,1:T(8,128)S(1)}, u32[]{:S(2)}, u32[]{:S(2)}) collective-permute-start(f32[2,2,1,8,128]{4,3,0,2,1:T(8,128)S(1)} %copy.355), channel_id=1, source_target_pairs={{0,16},{16,32},{32,48},{48,64},{64,80},{80,96},{96,112},{1,17},{17... | collective-permute-start | bytes 49160 | tf_op jit(solution)/shard_map/ppermute | solution.py:13
  202.0 2.2 collective-permute-start.19
  205.4 1.4 multiply_reduce_fusion
  207.5 1.3 maximum_bitcast_fusion
  208.8 63.8 %all-reduce.25.cloned.1.call-done = f32[16,8,128]{2,1,0:T(8,128)} async-done(((f32[16,8,128]{2,1,0:T(8,128)}), f32[16,8,128]{2,1,0:T(8,128)}) %all-reduce.25.cloned.1.call-update) | async-done | bytes 65552 | tf_op jit(solution)/shard_map/psum | solution.py:144
  272.6 1.5 copy.385
  (175 shorter events, 32.5 us)
Async XLA Ops:
  8.3 10.8 %collective-permute-start = (f32[2,2,1,8,128]{4,0,3,2,1:T(2,128)S(1)}, f32[2,2,1,8,128]{4,0,3,2,1:T(2,128)S(1)}, u32[]{:S(2)}, u32[]{:S(2)}) collective-permute-start(f32[2,2,1,8,128]{4,0,3,2,1:T(2,128)S(1)} %bitcast.361), channel_id=1, source_target_pairs={{16,0},{32,16},{48,32},{64,48},{80,64},{96,80},{112,96},{17,1},{33... | collective-permute-start | bytes 49160 | tf_op jit(solution)/shard_map/ppermute | solution.py:13
  9.6 9.5 %collective-permute-start.1 = (f32[2,2,16,1,128]{4,2,0,3,1:T(8,128)S(1)}, f32[2,2,16,1,128]{4,2,0,3,1:T(8,128)S(1)}, u32[]{:S(2)}, u32[]{:S(2)}) collective-permute-start(f32[2,2,16,1,128]{4,2,0,3,1:T(8,128)S(1)} %slice.625), channel_id=1, source_target_pairs={{1,0},{2,1},{3,2},{4,3},{5,4},{6,5},{7,6},{8,7},{9,8},{10,9},{11,1... | collective-permute-start | bytes 98312 | tf_op jit(solution)/shard_map/ppermute | solution.py:13
  18.8 11.5 %copy-start.12 = (f32[2,1,16,8,128]{4,3,2,0,1:T(8,128)}, f32[2,1,16,8,128]{4,3,2,0,1:T(8,128)S(1)}, u32[]{:S(2)}) copy-start(f32[2,1,16,8,128]{4,3,2,0,1:T(8,128)S(1)} %get-tuple-element.123) | copy-start | bytes 393220
  18.8 45.0 %copy-start.1 = (f32[2,3,16,8,128]{4,3,2,1,0:T(8,128)S(1)}, f32[2,3,16,8,128]{4,3,2,1,0:T(8,128)}, u32[]{:S(2)}) copy-start(f32[2,3,16,8,128]{4,3,2,1,0:T(8,128)} %param.14) | copy-start | bytes 1179652
  18.8 34.2 %copy-start.18 = (s32[1024]{0:T(1024)}, s32[1024]{0:T(1024)S(1)}, u32[]{:S(2)}) copy-start(s32[1024]{0:T(1024)S(1)} %pad_clamp_fusion) | copy-start | bytes 12292
  20.3 8.7 %collective-permute-start.2 = (f32[2,2,1,8,128]{4,0,3,2,1:T(2,128)S(1)}, f32[2,2,1,8,128]{4,0,3,2,1:T(2,128)S(1)}, u32[]{:S(2)}, u32[]{:S(2)}) collective-permute-start(f32[2,2,1,8,128]{4,0,3,2,1:T(2,128)S(1)} %bitcast.362), channel_id=1, source_target_pairs={{0,16},{16,32},{32,48},{48,64},{64,80},{80,96},{96,112},{1,17},{17... | collective-permute-start | bytes 49160 | tf_op jit(solution)/shard_map/ppermute | solution.py:13
  25.0 5.0 %collective-permute-start.3 = (f32[2,2,16,1,128]{4,2,0,3,1:T(8,128)S(1)}, f32[2,2,16,1,128]{4,2,0,3,1:T(8,128)S(1)}, u32[]{:S(2)}, u32[]{:S(2)}) collective-permute-start(f32[2,2,16,1,128]{4,2,0,3,1:T(8,128)S(1)} %slice.636), channel_id=1, source_target_pairs={{0,1},{1,2},{2,3},{3,4},{4,5},{5,6},{6,7},{7,8},{8,9},{9,10},{10,1... | collective-permute-start | bytes 98312 | tf_op jit(solution)/shard_map/ppermute | solution.py:13
  31.6 21.4 %collective-permute-start.4 = (f32[2,2,1,8,128]{4,2,0,3,1:T(1,128)S(1)}, f32[2,2,1,8,128]{4,2,0,3,1:T(1,128)S(1)}, u32[]{:S(2)}, u32[]{:S(2)}) collective-permute-start(f32[2,2,1,8,128]{4,2,0,3,1:T(1,128)S(1)} %slice.643), channel_id=1, source_target_pairs={{16,0},{32,16},{48,32},{64,48},{80,64},{96,80},{112,96},{17,1},{33... | collective-permute-start | bytes 49160 | tf_op jit(solution)/shard_map/ppermute | solution.py:13
  44.5 8.5 %collective-permute-start.5 = (f32[2,2,16,1,128]{4,2,0,3,1:T(8,128)S(1)}, f32[2,2,16,1,128]{4,2,0,3,1:T(8,128)S(1)}, u32[]{:S(2)}, u32[]{:S(2)}) collective-permute-start(f32[2,2,16,1,128]{4,2,0,3,1:T(8,128)S(1)} %slice.647), channel_id=1, source_target_pairs={{1,0},{2,1},{3,2},{4,3},{5,4},{6,5},{7,6},{8,7},{9,8},{10,9},{11,1... | collective-permute-start | bytes 98312 | tf_op jit(solution)/shard_map/ppermute | solution.py:13
  53.2 10.6 %copy-start.6 = (f32[2,1,16,8,128]{4,3,2,0,1:T(8,128)}, f32[2,1,16,8,128]{4,3,2,0,1:T(8,128)S(1)}, u32[]{:S(2)}) copy-start(f32[2,1,16,8,128]{4,3,2,0,1:T(8,128)S(1)} %copy.285) | copy-start | bytes 393220
  53.3 10.4 %copy-start.7 = (f32[2,1,16,8,128]{4,3,2,0,1:T(8,128)}, f32[2,1,16,8,128]{4,3,2,0,1:T(8,128)S(1)}, u32[]{:S(2)}) copy-start(f32[2,1,16,8,128]{4,3,2,0,1:T(8,128)S(1)} %fusion.102) | copy-start | bytes 393220
  53.7 8.9 %collective-permute-start.6 = (f32[2,2,1,8,128]{4,3,0,2,1:T(8,128)S(1)}, f32[2,2,1,8,128]{4,3,0,2,1:T(8,128)S(1)}, u32[]{:S(2)}, u32[]{:S(2)}) collective-permute-start(f32[2,2,1,8,128]{4,3,0,2,1:T(8,128)S(1)} %slice_bitcast_fusion.44), channel_id=1, source_target_pairs={{0,16},{16,32},{32,48},{48,64},{64,80},{80,96},{96,112},{1,17},{17... | collective-permute-start | bytes 49160 | tf_op jit(solution)/shard_map/ppermute | solution.py:13
  57.7 5.8 %collective-permute-start.7 = (f32[2,2,16,1,128]{4,3,2,0,1:T(1,128)S(1)}, f32[2,2,16,1,128]{4,3,2,0,1:T(1,128)S(1)}, u32[]{:S(2)}, u32[]{:S(2)}) collective-permute-start(f32[2,2,16,1,128]{4,3,2,0,1:T(1,128)S(1)} %slice.658), channel_id=1, source_target_pairs={{0,1},{1,2},{2,3},{3,4},{4,5},{5,6},{6,7},{7,8},{8,9},{9,10},{10,1... | collective-permute-start | bytes 98312 | tf_op jit(solution)/shard_map/ppermute | solution.py:13
  63.7 61.5 %copy-start.2 = (f32[2,1,16,8,128]{4,3,2,0,1:T(8,128)}, f32[2,1,16,8,128]{4,3,2,0,1:T(8,128)S(1)}, u32[]{:S(2)}) copy-start(f32[2,1,16,8,128]{4,3,2,0,1:T(8,128)S(1)} %get-tuple-element.33) | copy-start | bytes 393220
  63.7 61.5 %copy-start.4 = (f32[2,1,16,8,128]{4,3,2,0,1:T(8,128)}, f32[2,1,16,8,128]{4,3,2,0,1:T(8,128)S(1)}, u32[]{:S(2)}) copy-start(f32[2,1,16,8,128]{4,3,2,0,1:T(8,128)S(1)} %get-tuple-element.34) | copy-start | bytes 393220
  64.6 10.1 %copy-start.10 = (f32[2,16,8,128]{3,2,1,0:T(8,128)}, f32[2,16,8,128]{3,2,1,0:T(8,128)S(1)}, u32[]{:S(2)}) copy-start(f32[2,16,8,128]{3,2,1,0:T(8,128)S(1)} %get-tuple-element.46) | copy-start | bytes 393220
  64.6 11.4 %copy-start.11 = (f32[2,16,8,128]{3,2,1,0:T(8,128)}, f32[2,16,8,128]{3,2,1,0:T(8,128)S(1)}, u32[]{:S(2)}) copy-start(f32[2,16,8,128]{3,2,1,0:T(8,128)S(1)} %get-tuple-element.47) | copy-start | bytes 393220
  65.3 29.2 %collective-permute-start.8 = (f32[2,2,1,8,128]{4,3,0,2,1:T(8,128)}, f32[2,2,1,8,128]{4,3,0,2,1:T(8,128)}, u32[]{:S(2)}, u32[]{:S(2)}) collective-permute-start(f32[2,2,1,8,128]{4,3,0,2,1:T(8,128)} %slice_bitcast_fusion.41), channel_id=1, source_target_pairs={{16,0},{32,16},{48,32},{64,48},{80,64},{96,80},{112,96},{17,1},{33... | collective-permute-start | bytes 49160 | tf_op jit(solution)/shard_map/ppermute | solution.py:13
  67.2 6.0 %copy-start.8 = (f32[2,16,8,128]{3,2,1,0:T(8,128)}, f32[2,16,8,128]{3,2,1,0:T(8,128)S(1)}, u32[]{:S(2)}) copy-start(f32[2,16,8,128]{3,2,1,0:T(8,128)S(1)} %get-tuple-element.71) | copy-start | bytes 393220
  67.2 6.7 %copy-start.9 = (f32[2,16,8,128]{3,2,1,0:T(8,128)}, f32[2,16,8,128]{3,2,1,0:T(8,128)S(1)}, u32[]{:S(2)}) copy-start(f32[2,16,8,128]{3,2,1,0:T(8,128)S(1)} %get-tuple-element.72) | copy-start | bytes 393220
  70.6 25.3 %collective-permute-start.9 = (f32[2,2,16,1,128]{4,3,2,0,1:T(1,128)}, f32[2,2,16,1,128]{4,3,2,0,1:T(1,128)}, u32[]{:S(2)}, u32[]{:S(2)}) collective-permute-start(f32[2,2,16,1,128]{4,3,2,0,1:T(1,128)} %slice.669), channel_id=1, source_target_pairs={{1,0},{2,1},{3,2},{4,3},{5,4},{6,5},{7,6},{8,7},{9,8},{10,9},{11,1... | collective-permute-start | bytes 98312 | tf_op jit(solution)/shard_map/ppermute | solution.py:13
  71.9 23.3 %collective-permute-start.12 = (f32[2,2,1,8,128]{4,3,0,2,1:T(8,128)}, f32[2,2,1,8,128]{4,3,0,2,1:T(8,128)}, u32[]{:S(2)}, u32[]{:S(2)}) collective-permute-start(f32[2,2,1,8,128]{4,3,0,2,1:T(8,128)} %slice_bitcast_fusion.35), channel_id=1, source_target_pairs={{16,0},{32,16},{48,32},{64,48},{80,64},{96,80},{112,96},{17,1},{33... | collective-permute-start | bytes 49160 | tf_op jit(solution)/shard_map/ppermute | solution.py:13
  74.7 30.2 %collective-permute-start.13 = (f32[2,2,16,1,128]{4,3,2,0,1:T(1,128)}, f32[2,2,16,1,128]{4,3,2,0,1:T(1,128)}, u32[]{:S(2)}, u32[]{:S(2)}) collective-permute-start(f32[2,2,16,1,128]{4,3,2,0,1:T(1,128)} %slice.691), channel_id=1, source_target_pairs={{1,0},{2,1},{3,2},{4,3},{5,4},{6,5},{7,6},{8,7},{9,8},{10,9},{11,1... | collective-permute-start | bytes 98312 | tf_op jit(solution)/shard_map/ppermute | solution.py:13
  100.4 23.5 %collective-permute-start.10 = (f32[2,2,1,8,128]{4,3,0,2,1:T(8,128)S(1)}, f32[2,2,1,8,128]{4,3,0,2,1:T(8,128)S(1)}, u32[]{:S(2)}, u32[]{:S(2)}) collective-permute-start(f32[2,2,1,8,128]{4,3,0,2,1:T(8,128)S(1)} %slice_bitcast_fusion.38), channel_id=1, source_target_pairs={{0,16},{16,32},{32,48},{48,64},{64,80},{80,96},{96,112},{1,17},{17... | collective-permute-start | bytes 49160 | tf_op jit(solution)/shard_map/ppermute | solution.py:13
  106.9 98.5 %copy-start = (f32[2,3,16,8,128]{4,3,2,1,0:T(8,128)S(1)}, f32[2,3,16,8,128]{4,3,2,1,0:T(8,128)}, u32[]{:S(2)}) copy-start(f32[2,3,16,8,128]{4,3,2,1,0:T(8,128)} %param.12) | copy-start | bytes 1179652
  109.3 14.6 %collective-permute-start.11 = (f32[2,2,16,1,128]{4,3,2,0,1:T(1,128)S(1)}, f32[2,2,16,1,128]{4,3,2,0,1:T(1,128)S(1)}, u32[]{:S(2)}, u32[]{:S(2)}) collective-permute-start(f32[2,2,16,1,128]{4,3,2,0,1:T(1,128)S(1)} %slice.680), channel_id=1, source_target_pairs={{0,1},{1,2},{2,3},{3,4},{4,5},{5,6},{6,7},{7,8},{8,9},{9,10},{10,1... | collective-permute-start | bytes 98312 | tf_op jit(solution)/shard_map/ppermute | solution.py:13
  115.2 8.7 %collective-permute-start.14 = (f32[2,2,1,8,128]{4,3,0,2,1:T(8,128)S(1)}, f32[2,2,1,8,128]{4,3,0,2,1:T(8,128)S(1)}, u32[]{:S(2)}, u32[]{:S(2)}) collective-permute-start(f32[2,2,1,8,128]{4,3,0,2,1:T(8,128)S(1)} %copy.349), channel_id=1, source_target_pairs={{0,16},{16,32},{32,48},{48,64},{64,80},{80,96},{96,112},{1,17},{17... | collective-permute-start | bytes 49160 | tf_op jit(solution)/shard_map/ppermute | solution.py:13
  119.3 5.6 %collective-permute-start.15 = (f32[2,2,16,1,128]{4,2,0,3,1:T(8,128)S(1)}, f32[2,2,16,1,128]{4,2,0,3,1:T(8,128)S(1)}, u32[]{:S(2)}, u32[]{:S(2)}) collective-permute-start(f32[2,2,16,1,128]{4,2,0,3,1:T(8,128)S(1)} %copy.351), channel_id=1, source_target_pairs={{0,1},{1,2},{2,3},{3,4},{4,5},{5,6},{6,7},{7,8},{8,9},{9,10},{10,1... | collective-permute-start | bytes 98312 | tf_op jit(solution)/shard_map/ppermute | solution.py:13
  127.7 19.2 %copy-start.16 = (f32[16,2,3]{2,1,0:T(2,128)S(1)}, f32[16,2,3]{2,1,0:T(2,128)}, u32[]{:S(2)}) copy-start(f32[16,2,3]{2,1,0:T(2,128)} %gather_fusion) | copy-start | bytes 1156
  127.7 19.2 %copy-start.17 = (f32[16,2,3]{2,1,0:T(2,128)S(1)}, f32[16,2,3]{2,1,0:T(2,128)}, u32[]{:S(2)}) copy-start(f32[16,2,3]{2,1,0:T(2,128)} %gather_fusion.1) | copy-start | bytes 1156
  127.7 19.2 %copy-start.19 = (pred[16]{0:T(512)(128)(4,1)S(1)}, pred[16]{0:T(512)(128)(4,1)}, u32[]{:S(2)}) copy-start(pred[16]{0:T(512)(128)(4,1)} %compare_and_fusion) | copy-start | bytes 52
  127.7 77.7 %copy-start.3 = (f32[2,1,16,8,128]{4,3,2,0,1:T(8,128)S(1)}, f32[2,1,16,8,128]{4,3,2,0,1:T(8,128)}, u32[]{:S(2)}) copy-start(f32[2,1,16,8,128]{4,3,2,0,1:T(8,128)} %copy-done.2) | copy-start | bytes 393220
  127.7 77.7 %copy-start.5 = (f32[2,1,16,8,128]{4,3,2,0,1:T(8,128)S(1)}, f32[2,1,16,8,128]{4,3,2,0,1:T(8,128)}, u32[]{:S(2)}) copy-start(f32[2,1,16,8,128]{4,3,2,0,1:T(8,128)} %copy-done.4) | copy-start | bytes 393220
  127.7 79.1 %copy-start.13 = (f32[16,8,128]{2,1,0:T(8,128)S(1)}, f32[16,8,128]{2,1,0:T(8,128)}, u32[]{:S(2)}) copy-start(f32[16,8,128]{2,1,0:T(8,128)} %get-tuple-element.22) | copy-start | bytes 196612
  148.2 22.2 %all-to-all-start.2 = ((f32[2,16,2,3]{3,2,0,1:T(2,128)}), f32[2,16,2,3]{3,2,0,1:T(2,128)S(1)}, u32[]{:S(2)}, u32[]{:S(2)}) async-start(f32[2,16,2,3]{3,2,0,1:T(2,128)} %copy.335), calls=%async_computation.2 | async-start | bytes 65536 | tf_op jit(solution)/shard_map/all_to_all | solution.py:127
  170.3 15.2 %copy-start.14 = (f32[2,16,2,3]{3,2,0,1:T(2,128)}, f32[2,16,2,3]{3,2,0,1:T(2,128)S(1)}, u32[]{:S(2)}) copy-start(f32[2,16,2,3]{3,2,0,1:T(2,128)S(1)} %all-to-all-done.2) | copy-start | bytes 2308
  170.3 11.1 %all-to-all-start.1 = ((f32[2,16,2,3]{3,2,0,1:T(2,128)}), f32[2,16,2,3]{3,2,0,1:T(2,128)S(1)}, u32[]{:S(2)}, u32[]{:S(2)}) async-start(f32[2,16,2,3]{3,2,0,1:T(2,128)} %copy.332), calls=%async_computation.1 | async-start | bytes 65536 | tf_op jit(solution)/shard_map/all_to_all | solution.py:127
  174.4 20.1 %collective-permute-start.16 = (f32[2,2,1,8,128]{4,3,0,2,1:T(8,128)}, f32[2,2,1,8,128]{4,3,0,2,1:T(8,128)}, u32[]{:S(2)}, u32[]{:S(2)}) collective-permute-start(f32[2,2,1,8,128]{4,3,0,2,1:T(8,128)} %slice_bitcast_fusion.32), channel_id=1, source_target_pairs={{16,0},{32,16},{48,32},{64,48},{80,64},{96,80},{112,96},{17,1},{33... | collective-permute-start | bytes 49160 | tf_op jit(solution)/shard_map/ppermute | solution.py:13
  181.4 4.1 %copy-start.15 = (f32[2,16,2,3]{3,2,0,1:T(2,128)}, f32[2,16,2,3]{3,2,0,1:T(2,128)S(1)}, u32[]{:S(2)}) copy-start(f32[2,16,2,3]{3,2,0,1:T(2,128)S(1)} %all-to-all-done.1) | copy-start | bytes 2308
  181.4 11.7 %all-to-all-start = ((f32[2,16,2,3]{3,2,0,1:T(2,128)}), f32[2,16,2,3]{3,2,0,1:T(2,128)}, u32[]{:S(2)}, u32[]{:S(2)}) async-start(f32[2,16,2,3]{3,2,0,1:T(2,128)} %copy.329), calls=%async_computation | async-start | bytes 65536 | tf_op jit(solution)/shard_map/all_to_all | solution.py:127
  185.6 87.0 %all-reduce.25.cloned.1.call-start = ((), (), s32[]{:S(2)}) async-start(), calls=%async_computation.3 | async-start | bytes 131072 | tf_op jit(solution)/shard_map/psum | solution.py:144
  187.1 8.2 %collective-permute-start.17 = (f32[2,2,16,1,128]{4,3,2,0,1:T(1,128)}, f32[2,2,16,1,128]{4,3,2,0,1:T(1,128)}, u32[]{:S(2)}, u32[]{:S(2)}) collective-permute-start(f32[2,2,16,1,128]{4,3,2,0,1:T(1,128)} %slice.713), channel_id=1, source_target_pairs={{1,0},{2,1},{3,2},{4,3},{5,4},{6,5},{7,6},{8,7},{9,8},{10,9},{11,1... | collective-permute-start | bytes 98312 | tf_op jit(solution)/shard_map/ppermute | solution.py:13
  197.3 6.9 %collective-permute-start.18 = (f32[2,2,1,8,128]{4,3,0,2,1:T(8,128)S(1)}, f32[2,2,1,8,128]{4,3,0,2,1:T(8,128)S(1)}, u32[]{:S(2)}, u32[]{:S(2)}) collective-permute-start(f32[2,2,1,8,128]{4,3,0,2,1:T(8,128)S(1)} %copy.355), channel_id=1, source_target_pairs={{0,16},{16,32},{32,48},{48,64},{64,80},{80,96},{96,112},{1,17},{17... | collective-permute-start | bytes 49160 | tf_op jit(solution)/shard_map/ppermute | solution.py:13
  202.0 3.2 %collective-permute-start.19 = (f32[2,2,16,1,128]{4,3,2,1,0:T(1,128)S(1)}, f32[2,2,16,1,128]{4,3,2,1,0:T(1,128)S(1)}, u32[]{:S(2)}, u32[]{:S(2)}) collective-permute-start(f32[2,2,16,1,128]{4,3,2,1,0:T(1,128)S(1)} %slice.724), channel_id=1, source_target_pairs={{0,1},{1,2},{2,3},{3,4},{4,5},{5,6},{6,7},{7,8},{8,9},{9,10},{10,1... | collective-permute-start | bytes 98312 | tf_op jit(solution)/shard_map/ppermute | solution.py:13
Sparse Core Ops, SparseCore 0:
  207.6 64.9 all-reduce.24
where the time goes:
time: 284 us; the launch traced here: 281 us
  waiting for transfers between devices  82.6 us (29%)
  local copies, waits for them, and re-layouts  78.5 us (28%)
  starting transfers between devices  78.4 us (28%)
  other arithmetic  26.5 us (9%)
  between operations  15 us (5%)
    psum x1, waiting for transfers between devices, per_device(): total = lax.psum(local, 'src')  63.8 us
    ppermute x20, starting transfers between devices, passed_along(): return lax.ppermute(block, axis, route)  56.2 us
    add x3, local copies, waits for them, and re-layouts, per_device(): e_field = decay_use * e_field + gain_use * drive  35.4 us
    all_to_all x3, starting transfers between devices, per_device(): lax.all_to_all(jnp.transpose(placed, (0, 2, 3, 1)), 'lat', split_axis=1,...  22.2 us
    gather x3, local copies, waits for them, and re-layouts, per_device(): sampled = jnp.take(e_field.reshape(groups, 3, -1), cells, axis=2)  20.5 us
    all_to_all x3, waiting for transfers between devices, per_device(): lax.all_to_all(jnp.transpose(placed, (0, 2, 3, 1)), 'lat', split_axis=1,...  14.9 us
    squeeze x27, local copies, waits for them, and re-layouts, component(): return field[..., k, :, :, :]  6.66 us
    another operation x10, other arithmetic, curl_upper(): return jnp.stack([yz - zy, zx - xz, xy - yx], axis=-4)  6.36 us
  transfers between devices with their start and end apart: 24, of which 8 were waited for; matrix products, arithmetic and copies ran while one was open for 25% of the time, Pallas kernels for 0%

commit v1 on v0

--- a/solution.py
+++ b/solution.py
@@ -141,7 +141,7 @@
         if step > 0:
             lam_h, turned = leap(lam_e, lam_h, gain)
             lam_e = decay_use * lam_e - ch_coef * turned
-    total = lax.psum(local, "src")
+    total = jnp.sum(lax.all_gather(local, "src"), axis=0)
     return (total, line_samples)
 
 

time: 284 us -> 229 us (0.81)
  the two profiles are of different devices: /device:TPU:1 before, /device:TPU:89 now
where the time goes in v1:
time: 229 us; the launch traced here: 226 us
  starting transfers between devices  81.2 us (35%)
  local copies, waits for them, and re-layouts  77.3 us (34%)
  other arithmetic  26.4 us (12%)
  waiting for transfers between devices  20.1 us (9%)
  blocking collectives  19.5 us (9%)
    ppermute x20, starting transfers between devices, passed_along(): return lax.ppermute(block, axis, route)  58.5 us
    add x3, local copies, waits for them, and re-layouts, per_device(): e_field = decay_use * e_field + gain_use * drive  35.7 us
    all_to_all x3, starting transfers between devices, per_device(): lax.all_to_all(jnp.transpose(placed, (0, 2, 3, 1)), 'lat', split_axis=1,...  22.7 us
    gather x3, local copies, waits for them, and re-layouts, per_device(): sampled = jnp.take(e_field.reshape(groups, 3, -1), cells, axis=2)  20.5 us
    all_gather x1, blocking collectives, per_device(): total = jnp.sum(lax.all_gather(local, 'src'), axis=0)  19.5 us
    all_to_all x3, waiting for transfers between devices, per_device(): lax.all_to_all(jnp.transpose(placed, (0, 2, 3, 1)), 'lat', split_axis=1,...  10.9 us
    ppermute x20, waiting for transfers between devices, passed_along(): return lax.ppermute(block, axis, route)  9.17 us
    squeeze x27, local copies, waits for them, and re-layouts, component(): return field[..., k, :, :, :]  6.66 us
  transfers between devices with their start and end apart: 23, of which 6 were waited for; matrix products, arithmetic and copies ran while one was open for 31% of the time, Pallas kernels for 0%

profile of v1, /device:TPU:89, one launch (start us, length us, event | category | flops | bytes accessed | tf_op | source)
XLA Modules:
  0.0 226.1 jit_solution(9767252880703992162)
XLA Ops:
  1.7 2.1 collective-permute-start
  3.8 2.2 collective-permute-start.1
  8.4 1.2 compare_and_fusion
  11.5 1.5 multiply_divide_fusion.1
  15.4 4.4 %collective-permute-start.2 = (f32[2,2,1,8,128]{4,0,3,2,1:T(2,128)S(1)}, f32[2,2,1,8,128]{4,0,3,2,1:T(2,128)S(1)}, u32[]{:S(2)}, u32[]{:S(2)}) collective-permute-start(f32[2,2,1,8,128]{4,0,3,2,1:T(2,128)S(1)} %bitcast.364), channel_id=1, source_target_pairs={{0,16},{16,32},{32,48},{48,64},{64,80},{80,96},{96,112},{1,17},{17... | collective-permute-start | bytes 49160 | tf_op jit(solution)/shard_map/ppermute | solution.py:13
  19.9 3.1 %collective-permute-start.3 = (f32[2,2,16,1,128]{4,2,0,3,1:T(8,128)S(1)}, f32[2,2,16,1,128]{4,2,0,3,1:T(8,128)S(1)}, u32[]{:S(2)}, u32[]{:S(2)}) collective-permute-start(f32[2,2,16,1,128]{4,2,0,3,1:T(8,128)S(1)} %slice.636), channel_id=1, source_target_pairs={{0,1},{1,2},{2,3},{3,4},{4,5},{5,6},{6,7},{7,8},{8,9},{9,10},{10,1... | collective-permute-start | bytes 98312 | tf_op jit(solution)/shard_map/ppermute | solution.py:13
  23.0 2.5 %collective-permute-done.3 = f32[2,2,16,1,128]{4,2,0,3,1:T(8,128)S(1)} collective-permute-done((f32[2,2,16,1,128]{4,2,0,3,1:T(8,128)S(1)}, f32[2,2,16,1,128]{4,2,0,3,1:T(8,128)S(1)}, u32[]{:S(2)}, u32[]{:S(2)}) %collective-permute-start.3) | collective-permute-done | bytes 32800 | tf_op jit(solution)/shard_map/ppermute | solution.py:13
  25.7 1.2 multiply_add_fusion.2
  27.0 1.9 collective-permute-start.4
  29.0 11.5 %copy.327 = f32[2,3,16,8,128]{1,0,4,3,2:T(2,128)} copy(f32[2,3,16,8,128]{4,3,2,0,1:T(8,128)S(1)} %multiply_add_fusion.2) | data formatting | bytes 786432 | tf_op jit(solution)/shard_map/add | solution.py:123
  40.6 1.9 collective-permute-start.5
  42.8 6.9 %gather_fusion = f32[16,2,3]{2,1,0:T(2,128)} fusion(f32[2,3,16384]{1,0,2:T(2,128)} %bitcast.335, s32[1024]{0:T(1024)S(1)} %pad_clamp_fusion), kind=kCustom, calls=%fused_computation.clone | custom fusion | bytes 832 | tf_op jit(solution)/shard_map/jit(_take)/gather | solution.py:124
  50.4 4.6 %collective-permute-start.6 = (f32[2,2,1,8,128]{4,3,0,2,1:T(8,128)S(1)}, f32[2,2,1,8,128]{4,3,0,2,1:T(8,128)S(1)}, u32[]{:S(2)}, u32[]{:S(2)}) collective-permute-start(f32[2,2,1,8,128]{4,3,0,2,1:T(8,128)S(1)} %slice_bitcast_fusion.44), channel_id=1, source_target_pairs={{0,16},{16,32},{32,48},{48,64},{64,80},{80,96},{96,112},{1,17},{17... | collective-permute-start | bytes 49160 | tf_op jit(solution)/shard_map/ppermute | solution.py:13
  55.1 3.4 %collective-permute-start.7 = (f32[2,2,16,1,128]{4,3,2,0,1:T(1,128)S(1)}, f32[2,2,16,1,128]{4,3,2,0,1:T(1,128)S(1)}, u32[]{:S(2)}, u32[]{:S(2)}) collective-permute-start(f32[2,2,16,1,128]{4,3,2,0,1:T(1,128)S(1)} %slice.658), channel_id=1, source_target_pairs={{0,1},{1,2},{2,3},{3,4},{4,5},{5,6},{6,7},{7,8},{8,9},{9,10},{10,1... | collective-permute-start | bytes 98312 | tf_op jit(solution)/shard_map/ppermute | solution.py:13
  58.5 2.2 collective-permute-done.7
  62.3 1.9 collective-permute-start.8
  68.4 1.9 collective-permute-start.9
  70.3 1.9 collective-permute-start.12
  73.7 1.9 collective-permute-start.13
  75.7 11.5 %copy.330 = f32[2,3,16,8,128]{1,0,4,3,2:T(2,128)} copy(f32[2,3,16,8,128]{4,3,2,0,1:T(8,128)S(1)} %get-tuple-element.18) | data formatting | bytes 786432 | tf_op jit(solution)/shard_map/add | solution.py:123
  87.1 7.1 %gather_fusion.1 = f32[16,2,3]{2,1,0:T(2,128)} fusion(f32[2,3,16384]{1,0,2:T(2,128)} %bitcast.337, s32[1024]{0:T(1024)} %copy-done.18), kind=kCustom, calls=%fused_computation.1.clone | custom fusion | bytes 832 | tf_op jit(solution)/shard_map/jit(_take)/gather | solution.py:124
  96.4 1.1 fusion.59
  97.5 1.2 fusion.63
  98.8 1.2 maximum_add_fusion.2
  100.1 4.6 %collective-permute-start.10 = (f32[2,2,1,8,128]{4,3,0,2,1:T(8,128)S(1)}, f32[2,2,1,8,128]{4,3,0,2,1:T(8,128)S(1)}, u32[]{:S(2)}, u32[]{:S(2)}) collective-permute-start(f32[2,2,1,8,128]{4,3,0,2,1:T(8,128)S(1)} %slice_bitcast_fusion.38), channel_id=1, source_target_pairs={{0,16},{16,32},{32,48},{48,64},{64,80},{80,96},{96,112},{1,17},{17... | collective-permute-start | bytes 49160 | tf_op jit(solution)/shard_map/ppermute | solution.py:13
  105.4 1.1 fusion.39
  106.5 1.3 fusion.43
  109.0 3.4 %collective-permute-start.11 = (f32[2,2,16,1,128]{4,3,2,0,1:T(1,128)S(1)}, f32[2,2,16,1,128]{4,3,2,0,1:T(1,128)S(1)}, u32[]{:S(2)}, u32[]{:S(2)}) collective-permute-start(f32[2,2,16,1,128]{4,3,2,0,1:T(1,128)S(1)} %slice.680), channel_id=1, source_target_pairs={{0,1},{1,2},{2,3},{3,4},{4,5},{5,6},{6,7},{7,8},{8,9},{9,10},{10,1... | collective-permute-start | bytes 98312 | tf_op jit(solution)/shard_map/ppermute | solution.py:13
  112.4 3.4 %collective-permute-start.14 = (f32[2,2,1,8,128]{4,3,0,2,1:T(8,128)S(1)}, f32[2,2,1,8,128]{4,3,0,2,1:T(8,128)S(1)}, u32[]{:S(2)}, u32[]{:S(2)}) collective-permute-start(f32[2,2,1,8,128]{4,3,0,2,1:T(8,128)S(1)} %copy.349), channel_id=1, source_target_pairs={{0,16},{16,32},{32,48},{48,64},{64,80},{80,96},{96,112},{1,17},{17... | collective-permute-start | bytes 49160 | tf_op jit(solution)/shard_map/ppermute | solution.py:13
  115.8 4.3 %collective-permute-start.15 = (f32[2,2,16,1,128]{4,2,0,3,1:T(8,128)S(1)}, f32[2,2,16,1,128]{4,2,0,3,1:T(8,128)S(1)}, u32[]{:S(2)}, u32[]{:S(2)}) collective-permute-start(f32[2,2,16,1,128]{4,2,0,3,1:T(8,128)S(1)} %copy.351), channel_id=1, source_target_pairs={{0,1},{1,2},{2,3},{3,4},{4,5},{5,6},{6,7},{7,8},{8,9},{9,10},{10,1... | collective-permute-start | bytes 98312 | tf_op jit(solution)/shard_map/ppermute | solution.py:13
  120.2 1.2 collective-permute-done.15
  121.7 2.5 %multiply_add_fusion = (f32[2,3,16,8,128]{4,3,2,0,1:T(8,128)}, f32[16,8,128]{2,1,0:T(8,128)}, f32[2,3,16,8,128]{4,3,2,0,1:T(8,128)S(1)}, f32[2,3,16,8,128]{4,3,2,0,1:T(8,128)S(1)}) fusion(f32[2,3,16,8,128]{4,3,2,0,1:T(8,128)S(1)} %get-tuple-element.18, f32[16,8,128]{2,1,0:T(8,128)S(1)} %get-tuple-element.80, f32[16,8,128]{2,1,0:T(8,128)S(1)} %get-tuple-element.78, ...), kind=kLoop, calls=%fused_computation.24 | loop fusion | flops 1654784 | bytes 3211264 | tf_op jit(solution)/shard_map/add | solution.py:123
  124.2 12.7 %copy.333 = f32[2,3,16,8,128]{1,0,4,3,2:T(2,128)} copy(f32[2,3,16,8,128]{4,3,2,0,1:T(8,128)} %get-tuple-element.21) | data formatting | bytes 786432 | tf_op jit(solution)/shard_map/add | solution.py:123
  137.0 6.5 %gather_fusion.2 = f32[16,2,3]{2,1,0:T(2,128)S(1)} fusion(f32[2,3,16384]{1,0,2:T(2,128)} %bitcast.336, s32[1024]{0:T(1024)} %copy-done.18), kind=kCustom, calls=%fused_computation.2.clone | custom fusion | bytes 832 | tf_op jit(solution)/shard_map/jit(_take)/gather | solution.py:124
  144.7 13.0 %all-to-all-start.2 = ((f32[2,16,2,3]{3,2,0,1:T(2,128)}), f32[2,16,2,3]{3,2,0,1:T(2,128)S(1)}, u32[]{:S(2)}, u32[]{:S(2)}) async-start(f32[2,16,2,3]{3,2,0,1:T(2,128)} %copy.335), calls=%async_computation.2 | async-start | bytes 65536 | tf_op jit(solution)/shard_map/all_to_all | solution.py:127
  158.4 5.8 %all-to-all-done.2 = f32[2,16,2,3]{3,2,0,1:T(2,128)S(1)} async-done(((f32[2,16,2,3]{3,2,0,1:T(2,128)}), f32[2,16,2,3]{3,2,0,1:T(2,128)S(1)}, u32[]{:S(2)}, u32[]{:S(2)}) %all-to-all-start.2) | async-done | bytes 800 | tf_op jit(solution)/shard_map/all_to_all | solution.py:127
  164.2 4.5 %all-to-all-start.1 = ((f32[2,16,2,3]{3,2,0,1:T(2,128)}), f32[2,16,2,3]{3,2,0,1:T(2,128)S(1)}, u32[]{:S(2)}, u32[]{:S(2)}) async-start(f32[2,16,2,3]{3,2,0,1:T(2,128)} %copy.332), calls=%async_computation.1 | async-start | bytes 65536 | tf_op jit(solution)/shard_map/all_to_all | solution.py:127
  170.1 5.1 %all-to-all-done.1 = f32[2,16,2,3]{3,2,0,1:T(2,128)S(1)} async-done(((f32[2,16,2,3]{3,2,0,1:T(2,128)}), f32[2,16,2,3]{3,2,0,1:T(2,128)S(1)}, u32[]{:S(2)}, u32[]{:S(2)}) %all-to-all-start.1) | async-done | bytes 800 | tf_op jit(solution)/shard_map/all_to_all | solution.py:127
  175.3 5.1 %all-to-all-start = ((f32[2,16,2,3]{3,2,0,1:T(2,128)}), f32[2,16,2,3]{3,2,0,1:T(2,128)}, u32[]{:S(2)}, u32[]{:S(2)}) async-start(f32[2,16,2,3]{3,2,0,1:T(2,128)} %copy.329), calls=%async_computation | async-start | bytes 65536 | tf_op jit(solution)/shard_map/all_to_all | solution.py:127
  181.7 1.9 collective-permute-start.16
  183.8 3.1 %collective-permute-start.17 = (f32[2,2,16,1,128]{4,3,2,0,1:T(1,128)}, f32[2,2,16,1,128]{4,3,2,0,1:T(1,128)}, u32[]{:S(2)}, u32[]{:S(2)}) collective-permute-start(f32[2,2,16,1,128]{4,3,2,0,1:T(1,128)} %slice.713), channel_id=1, source_target_pairs={{1,0},{2,1},{3,2},{4,3},{5,4},{6,5},{7,6},{8,7},{9,8},{10,9},{11,1... | collective-permute-start | bytes 98312 | tf_op jit(solution)/shard_map/ppermute | solution.py:13
  188.6 1.4 copy.336
  190.0 1.3 maximum_bitcast_fusion
  194.1 4.6 %collective-permute-start.18 = (f32[2,2,1,8,128]{4,3,0,2,1:T(8,128)S(1)}, f32[2,2,1,8,128]{4,3,0,2,1:T(8,128)S(1)}, u32[]{:S(2)}, u32[]{:S(2)}) collective-permute-start(f32[2,2,1,8,128]{4,3,0,2,1:T(8,128)S(1)} %copy.355), channel_id=1, source_target_pairs={{0,16},{16,32},{32,48},{48,64},{64,80},{80,96},{96,112},{1,17},{17... | collective-permute-start | bytes 49160 | tf_op jit(solution)/shard_map/ppermute | solution.py:13
  198.7 2.2 collective-permute-start.19
  201.0 3.3 %collective-permute-done.19 = f32[2,2,16,1,128]{4,3,2,1,0:T(1,128)S(1)} collective-permute-done((f32[2,2,16,1,128]{4,3,2,1,0:T(1,128)S(1)}, f32[2,2,16,1,128]{4,3,2,1,0:T(1,128)S(1)}, u32[]{:S(2)}, u32[]{:S(2)}) %collective-permute-start.19) | collective-permute-done | bytes 32800 | tf_op jit(solution)/shard_map/ppermute | solution.py:13
  204.5 1.4 multiply_reduce_fusion
  205.9 19.5 %all-gather = f32[64,8,128]{2,1,0:T(8,128)S(1)} all-gather(f32[16,8,128]{2,1,0:T(8,128)S(1)} %add_add_fusion), channel_id=2, replica_groups=mesh['src'=4,'depth'=8,'lat'=16] {'src'}, dimensions={0}, use_global_device_ids=true | all-gather | bytes 327680 | tf_op jit(solution)/shard_map/all_gather | solution.py:144
  (173 shorter events, 31.0 us)
Async XLA Ops:
  1.7 12.4 %collective-permute-start = (f32[2,2,1,8,128]{4,0,3,2,1:T(2,128)S(1)}, f32[2,2,1,8,128]{4,0,3,2,1:T(2,128)S(1)}, u32[]{:S(2)}, u32[]{:S(2)}) collective-permute-start(f32[2,2,1,8,128]{4,0,3,2,1:T(2,128)S(1)} %bitcast.363), channel_id=1, source_target_pairs={{16,0},{32,16},{48,32},{64,48},{80,64},{96,80},{112,96},{17,1},{33... | collective-permute-start | bytes 49160 | tf_op jit(solution)/shard_map/ppermute | solution.py:13
  3.8 10.3 %collective-permute-start.1 = (f32[2,2,16,1,128]{4,2,0,3,1:T(8,128)S(1)}, f32[2,2,16,1,128]{4,2,0,3,1:T(8,128)S(1)}, u32[]{:S(2)}, u32[]{:S(2)}) collective-permute-start(f32[2,2,16,1,128]{4,2,0,3,1:T(8,128)S(1)} %slice.625), channel_id=1, source_target_pairs={{1,0},{2,1},{3,2},{4,3},{5,4},{6,5},{7,6},{8,7},{9,8},{10,9},{11,1... | collective-permute-start | bytes 98312 | tf_op jit(solution)/shard_map/ppermute | solution.py:13
  13.9 11.8 %copy-start.12 = (f32[2,1,16,8,128]{4,3,2,0,1:T(8,128)}, f32[2,1,16,8,128]{4,3,2,0,1:T(8,128)S(1)}, u32[]{:S(2)}) copy-start(f32[2,1,16,8,128]{4,3,2,0,1:T(8,128)S(1)} %get-tuple-element.123) | copy-start | bytes 393220
  13.9 47.0 %copy-start.1 = (f32[2,3,16,8,128]{4,3,2,1,0:T(8,128)S(1)}, f32[2,3,16,8,128]{4,3,2,1,0:T(8,128)}, u32[]{:S(2)}) copy-start(f32[2,3,16,8,128]{4,3,2,1,0:T(8,128)} %param.14) | copy-start | bytes 1179652
  13.9 35.9 %copy-start.18 = (s32[1024]{0:T(1024)}, s32[1024]{0:T(1024)S(1)}, u32[]{:S(2)}) copy-start(s32[1024]{0:T(1024)S(1)} %pad_clamp_fusion) | copy-start | bytes 12292
  15.4 7.6 %collective-permute-start.2 = (f32[2,2,1,8,128]{4,0,3,2,1:T(2,128)S(1)}, f32[2,2,1,8,128]{4,0,3,2,1:T(2,128)S(1)}, u32[]{:S(2)}, u32[]{:S(2)}) collective-permute-start(f32[2,2,1,8,128]{4,0,3,2,1:T(2,128)S(1)} %bitcast.364), channel_id=1, source_target_pairs={{0,16},{16,32},{32,48},{48,64},{64,80},{80,96},{96,112},{1,17},{17... | collective-permute-start | bytes 49160 | tf_op jit(solution)/shard_map/ppermute | solution.py:13
  19.9 5.6 %collective-permute-start.3 = (f32[2,2,16,1,128]{4,2,0,3,1:T(8,128)S(1)}, f32[2,2,16,1,128]{4,2,0,3,1:T(8,128)S(1)}, u32[]{:S(2)}, u32[]{:S(2)}) collective-permute-start(f32[2,2,16,1,128]{4,2,0,3,1:T(8,128)S(1)} %slice.636), channel_id=1, source_target_pairs={{0,1},{1,2},{2,3},{3,4},{4,5},{5,6},{6,7},{7,8},{8,9},{9,10},{10,1... | collective-permute-start | bytes 98312 | tf_op jit(solution)/shard_map/ppermute | solution.py:13
  27.0 22.7 %collective-permute-start.4 = (f32[2,2,1,8,128]{4,2,0,3,1:T(1,128)S(1)}, f32[2,2,1,8,128]{4,2,0,3,1:T(1,128)S(1)}, u32[]{:S(2)}, u32[]{:S(2)}) collective-permute-start(f32[2,2,1,8,128]{4,2,0,3,1:T(1,128)S(1)} %slice.643), channel_id=1, source_target_pairs={{16,0},{32,16},{48,32},{64,48},{80,64},{96,80},{112,96},{17,1},{33... | collective-permute-start | bytes 49160 | tf_op jit(solution)/shard_map/ppermute | solution.py:13
  40.6 9.2 %collective-permute-start.5 = (f32[2,2,16,1,128]{4,2,0,3,1:T(8,128)S(1)}, f32[2,2,16,1,128]{4,2,0,3,1:T(8,128)S(1)}, u32[]{:S(2)}, u32[]{:S(2)}) collective-permute-start(f32[2,2,16,1,128]{4,2,0,3,1:T(8,128)S(1)} %slice.647), channel_id=1, source_target_pairs={{1,0},{2,1},{3,2},{4,3},{5,4},{6,5},{7,6},{8,7},{9,8},{10,9},{11,1... | collective-permute-start | bytes 98312 | tf_op jit(solution)/shard_map/ppermute | solution.py:13
  49.9 10.9 %copy-start.6 = (f32[2,1,16,8,128]{4,3,2,0,1:T(8,128)}, f32[2,1,16,8,128]{4,3,2,0,1:T(8,128)S(1)}, u32[]{:S(2)}) copy-start(f32[2,1,16,8,128]{4,3,2,0,1:T(8,128)S(1)} %copy.285) | copy-start | bytes 393220
  50.1 10.8 %copy-start.7 = (f32[2,1,16,8,128]{4,3,2,0,1:T(8,128)}, f32[2,1,16,8,128]{4,3,2,0,1:T(8,128)S(1)}, u32[]{:S(2)}) copy-start(f32[2,1,16,8,128]{4,3,2,0,1:T(8,128)S(1)} %fusion.102) | copy-start | bytes 393220
  50.4 8.0 %collective-permute-start.6 = (f32[2,2,1,8,128]{4,3,0,2,1:T(8,128)S(1)}, f32[2,2,1,8,128]{4,3,0,2,1:T(8,128)S(1)}, u32[]{:S(2)}, u32[]{:S(2)}) collective-permute-start(f32[2,2,1,8,128]{4,3,0,2,1:T(8,128)S(1)} %slice_bitcast_fusion.44), channel_id=1, source_target_pairs={{0,16},{16,32},{32,48},{48,64},{64,80},{80,96},{96,112},{1,17},{17... | collective-permute-start | bytes 49160 | tf_op jit(solution)/shard_map/ppermute | solution.py:13
  55.1 5.6 %collective-permute-start.7 = (f32[2,2,16,1,128]{4,3,2,0,1:T(1,128)S(1)}, f32[2,2,16,1,128]{4,3,2,0,1:T(1,128)S(1)}, u32[]{:S(2)}, u32[]{:S(2)}) collective-permute-start(f32[2,2,16,1,128]{4,3,2,0,1:T(1,128)S(1)} %slice.658), channel_id=1, source_target_pairs={{0,1},{1,2},{2,3},{3,4},{4,5},{5,6},{6,7},{7,8},{8,9},{9,10},{10,1... | collective-permute-start | bytes 98312 | tf_op jit(solution)/shard_map/ppermute | solution.py:13
  60.8 60.8 %copy-start.2 = (f32[2,1,16,8,128]{4,3,2,0,1:T(8,128)}, f32[2,1,16,8,128]{4,3,2,0,1:T(8,128)S(1)}, u32[]{:S(2)}) copy-start(f32[2,1,16,8,128]{4,3,2,0,1:T(8,128)S(1)} %get-tuple-element.33) | copy-start | bytes 393220
  60.8 60.8 %copy-start.4 = (f32[2,1,16,8,128]{4,3,2,0,1:T(8,128)}, f32[2,1,16,8,128]{4,3,2,0,1:T(8,128)S(1)}, u32[]{:S(2)}) copy-start(f32[2,1,16,8,128]{4,3,2,0,1:T(8,128)S(1)} %get-tuple-element.34) | copy-start | bytes 393220
  61.7 12.1 %copy-start.10 = (f32[2,16,8,128]{3,2,1,0:T(8,128)}, f32[2,16,8,128]{3,2,1,0:T(8,128)S(1)}, u32[]{:S(2)}) copy-start(f32[2,16,8,128]{3,2,1,0:T(8,128)S(1)} %get-tuple-element.46) | copy-start | bytes 393220
  61.7 14.0 %copy-start.11 = (f32[2,16,8,128]{3,2,1,0:T(8,128)}, f32[2,16,8,128]{3,2,1,0:T(8,128)S(1)}, u32[]{:S(2)}) copy-start(f32[2,16,8,128]{3,2,1,0:T(8,128)S(1)} %get-tuple-element.47) | copy-start | bytes 393220
  62.3 31.9 %collective-permute-start.8 = (f32[2,2,1,8,128]{4,3,0,2,1:T(8,128)}, f32[2,2,1,8,128]{4,3,0,2,1:T(8,128)}, u32[]{:S(2)}, u32[]{:S(2)}) collective-permute-start(f32[2,2,1,8,128]{4,3,0,2,1:T(8,128)} %slice_bitcast_fusion.41), channel_id=1, source_target_pairs={{16,0},{32,16},{48,32},{64,48},{80,64},{96,80},{112,96},{17,1},{33... | collective-permute-start | bytes 49160 | tf_op jit(solution)/shard_map/ppermute | solution.py:13
  64.9 7.3 %copy-start.8 = (f32[2,16,8,128]{3,2,1,0:T(8,128)}, f32[2,16,8,128]{3,2,1,0:T(8,128)S(1)}, u32[]{:S(2)}) copy-start(f32[2,16,8,128]{3,2,1,0:T(8,128)S(1)} %get-tuple-element.71) | copy-start | bytes 393220
  64.9 8.0 %copy-start.9 = (f32[2,16,8,128]{3,2,1,0:T(8,128)}, f32[2,16,8,128]{3,2,1,0:T(8,128)S(1)}, u32[]{:S(2)}) copy-start(f32[2,16,8,128]{3,2,1,0:T(8,128)S(1)} %get-tuple-element.72) | copy-start | bytes 393220
  68.4 27.3 %collective-permute-start.9 = (f32[2,2,16,1,128]{4,3,2,0,1:T(1,128)}, f32[2,2,16,1,128]{4,3,2,0,1:T(1,128)}, u32[]{:S(2)}, u32[]{:S(2)}) collective-permute-start(f32[2,2,16,1,128]{4,3,2,0,1:T(1,128)} %slice.669), channel_id=1, source_target_pairs={{1,0},{2,1},{3,2},{4,3},{5,4},{6,5},{7,6},{8,7},{9,8},{10,9},{11,1... | collective-permute-start | bytes 98312 | tf_op jit(solution)/shard_map/ppermute | solution.py:13
  70.3 24.7 %collective-permute-start.12 = (f32[2,2,1,8,128]{4,3,0,2,1:T(8,128)}, f32[2,2,1,8,128]{4,3,0,2,1:T(8,128)}, u32[]{:S(2)}, u32[]{:S(2)}) collective-permute-start(f32[2,2,1,8,128]{4,3,0,2,1:T(8,128)} %slice_bitcast_fusion.35), channel_id=1, source_target_pairs={{16,0},{32,16},{48,32},{64,48},{80,64},{96,80},{112,96},{17,1},{33... | collective-permute-start | bytes 49160 | tf_op jit(solution)/shard_map/ppermute | solution.py:13
  73.7 30.9 %collective-permute-start.13 = (f32[2,2,16,1,128]{4,3,2,0,1:T(1,128)}, f32[2,2,16,1,128]{4,3,2,0,1:T(1,128)}, u32[]{:S(2)}, u32[]{:S(2)}) collective-permute-start(f32[2,2,16,1,128]{4,3,2,0,1:T(1,128)} %slice.691), channel_id=1, source_target_pairs={{1,0},{2,1},{3,2},{4,3},{5,4},{6,5},{7,6},{8,7},{9,8},{10,9},{11,1... | collective-permute-start | bytes 98312 | tf_op jit(solution)/shard_map/ppermute | solution.py:13
  100.1 20.0 %collective-permute-start.10 = (f32[2,2,1,8,128]{4,3,0,2,1:T(8,128)S(1)}, f32[2,2,1,8,128]{4,3,0,2,1:T(8,128)S(1)}, u32[]{:S(2)}, u32[]{:S(2)}) collective-permute-start(f32[2,2,1,8,128]{4,3,0,2,1:T(8,128)S(1)} %slice_bitcast_fusion.38), channel_id=1, source_target_pairs={{0,16},{16,32},{32,48},{48,64},{64,80},{80,96},{96,112},{1,17},{17... | collective-permute-start | bytes 49160 | tf_op jit(solution)/shard_map/ppermute | solution.py:13
  106.5 98.0 %copy-start = (f32[2,3,16,8,128]{4,3,2,1,0:T(8,128)S(1)}, f32[2,3,16,8,128]{4,3,2,1,0:T(8,128)}, u32[]{:S(2)}) copy-start(f32[2,3,16,8,128]{4,3,2,1,0:T(8,128)} %param.12) | copy-start | bytes 1179652
  109.0 11.1 %collective-permute-start.11 = (f32[2,2,16,1,128]{4,3,2,0,1:T(1,128)S(1)}, f32[2,2,16,1,128]{4,3,2,0,1:T(1,128)S(1)}, u32[]{:S(2)}, u32[]{:S(2)}) collective-permute-start(f32[2,2,16,1,128]{4,3,2,0,1:T(1,128)S(1)} %slice.680), channel_id=1, source_target_pairs={{0,1},{1,2},{2,3},{3,4},{4,5},{5,6},{6,7},{7,8},{8,9},{9,10},{10,1... | collective-permute-start | bytes 98312 | tf_op jit(solution)/shard_map/ppermute | solution.py:13
  112.4 7.7 %collective-permute-start.14 = (f32[2,2,1,8,128]{4,3,0,2,1:T(8,128)S(1)}, f32[2,2,1,8,128]{4,3,0,2,1:T(8,128)S(1)}, u32[]{:S(2)}, u32[]{:S(2)}) collective-permute-start(f32[2,2,1,8,128]{4,3,0,2,1:T(8,128)S(1)} %copy.349), channel_id=1, source_target_pairs={{0,16},{16,32},{32,48},{48,64},{64,80},{80,96},{96,112},{1,17},{17... | collective-permute-start | bytes 49160 | tf_op jit(solution)/shard_map/ppermute | solution.py:13
  115.8 5.6 %collective-permute-start.15 = (f32[2,2,16,1,128]{4,2,0,3,1:T(8,128)S(1)}, f32[2,2,16,1,128]{4,2,0,3,1:T(8,128)S(1)}, u32[]{:S(2)}, u32[]{:S(2)}) collective-permute-start(f32[2,2,16,1,128]{4,2,0,3,1:T(8,128)S(1)} %copy.351), channel_id=1, source_target_pairs={{0,1},{1,2},{2,3},{3,4},{4,5},{5,6},{6,7},{7,8},{8,9},{9,10},{10,1... | collective-permute-start | bytes 98312 | tf_op jit(solution)/shard_map/ppermute | solution.py:13
  124.2 19.2 %copy-start.16 = (f32[16,2,3]{2,1,0:T(2,128)S(1)}, f32[16,2,3]{2,1,0:T(2,128)}, u32[]{:S(2)}) copy-start(f32[16,2,3]{2,1,0:T(2,128)} %gather_fusion) | copy-start | bytes 1156
  124.2 19.2 %copy-start.17 = (f32[16,2,3]{2,1,0:T(2,128)S(1)}, f32[16,2,3]{2,1,0:T(2,128)}, u32[]{:S(2)}) copy-start(f32[16,2,3]{2,1,0:T(2,128)} %gather_fusion.1) | copy-start | bytes 1156
  124.2 19.2 %copy-start.19 = (pred[16]{0:T(512)(128)(4,1)S(1)}, pred[16]{0:T(512)(128)(4,1)}, u32[]{:S(2)}) copy-start(pred[16]{0:T(512)(128)(4,1)} %compare_and_fusion) | copy-start | bytes 52
  124.2 80.3 %copy-start.3 = (f32[2,1,16,8,128]{4,3,2,0,1:T(8,128)S(1)}, f32[2,1,16,8,128]{4,3,2,0,1:T(8,128)}, u32[]{:S(2)}) copy-start(f32[2,1,16,8,128]{4,3,2,0,1:T(8,128)} %copy-done.2) | copy-start | bytes 393220
  124.2 80.3 %copy-start.5 = (f32[2,1,16,8,128]{4,3,2,0,1:T(8,128)S(1)}, f32[2,1,16,8,128]{4,3,2,0,1:T(8,128)}, u32[]{:S(2)}) copy-start(f32[2,1,16,8,128]{4,3,2,0,1:T(8,128)} %copy-done.4) | copy-start | bytes 393220
  124.2 81.7 %copy-start.13 = (f32[16,8,128]{2,1,0:T(8,128)S(1)}, f32[16,8,128]{2,1,0:T(8,128)}, u32[]{:S(2)}) copy-start(f32[16,8,128]{2,1,0:T(8,128)} %get-tuple-element.22) | copy-start | bytes 196612
  144.7 19.5 %all-to-all-start.2 = ((f32[2,16,2,3]{3,2,0,1:T(2,128)}), f32[2,16,2,3]{3,2,0,1:T(2,128)S(1)}, u32[]{:S(2)}, u32[]{:S(2)}) async-start(f32[2,16,2,3]{3,2,0,1:T(2,128)} %copy.335), calls=%async_computation.2 | async-start | bytes 65536 | tf_op jit(solution)/shard_map/all_to_all | solution.py:127
  164.2 4.5 %copy-start.14 = (f32[2,16,2,3]{3,2,0,1:T(2,128)}, f32[2,16,2,3]{3,2,0,1:T(2,128)S(1)}, u32[]{:S(2)}) copy-start(f32[2,16,2,3]{3,2,0,1:T(2,128)S(1)} %all-to-all-done.2) | copy-start | bytes 2308
  164.2 11.1 %all-to-all-start.1 = ((f32[2,16,2,3]{3,2,0,1:T(2,128)}), f32[2,16,2,3]{3,2,0,1:T(2,128)S(1)}, u32[]{:S(2)}, u32[]{:S(2)}) async-start(f32[2,16,2,3]{3,2,0,1:T(2,128)} %copy.332), calls=%async_computation.1 | async-start | bytes 65536 | tf_op jit(solution)/shard_map/all_to_all | solution.py:127
  175.3 8.3 %copy-start.15 = (f32[2,16,2,3]{3,2,0,1:T(2,128)}, f32[2,16,2,3]{3,2,0,1:T(2,128)S(1)}, u32[]{:S(2)}) copy-start(f32[2,16,2,3]{3,2,0,1:T(2,128)S(1)} %all-to-all-done.1) | copy-start | bytes 2308
  175.3 13.3 %all-to-all-start = ((f32[2,16,2,3]{3,2,0,1:T(2,128)}), f32[2,16,2,3]{3,2,0,1:T(2,128)}, u32[]{:S(2)}, u32[]{:S(2)}) async-start(f32[2,16,2,3]{3,2,0,1:T(2,128)} %copy.329), calls=%async_computation | async-start | bytes 65536 | tf_op jit(solution)/shard_map/all_to_all | solution.py:127
  181.7 9.7 %collective-permute-start.16 = (f32[2,2,1,8,128]{4,3,0,2,1:T(8,128)}, f32[2,2,1,8,128]{4,3,0,2,1:T(8,128)}, u32[]{:S(2)}, u32[]{:S(2)}) collective-permute-start(f32[2,2,1,8,128]{4,3,0,2,1:T(8,128)} %slice_bitcast_fusion.32), channel_id=1, source_target_pairs={{16,0},{32,16},{48,32},{64,48},{80,64},{96,80},{112,96},{17,1},{33... | collective-permute-start | bytes 49160 | tf_op jit(solution)/shard_map/ppermute | solution.py:13
  183.8 8.3 %collective-permute-start.17 = (f32[2,2,16,1,128]{4,3,2,0,1:T(1,128)}, f32[2,2,16,1,128]{4,3,2,0,1:T(1,128)}, u32[]{:S(2)}, u32[]{:S(2)}) collective-permute-start(f32[2,2,16,1,128]{4,3,2,0,1:T(1,128)} %slice.713), channel_id=1, source_target_pairs={{1,0},{2,1},{3,2},{4,3},{5,4},{6,5},{7,6},{8,7},{9,8},{10,9},{11,1... | collective-permute-start | bytes 98312 | tf_op jit(solution)/shard_map/ppermute | solution.py:13
  194.1 6.9 %collective-permute-start.18 = (f32[2,2,1,8,128]{4,3,0,2,1:T(8,128)S(1)}, f32[2,2,1,8,128]{4,3,0,2,1:T(8,128)S(1)}, u32[]{:S(2)}, u32[]{:S(2)}) collective-permute-start(f32[2,2,1,8,128]{4,3,0,2,1:T(8,128)S(1)} %copy.355), channel_id=1, source_target_pairs={{0,16},{16,32},{32,48},{48,64},{64,80},{80,96},{96,112},{1,17},{17... | collective-permute-start | bytes 49160 | tf_op jit(solution)/shard_map/ppermute | solution.py:13
  198.7 5.6 %collective-permute-start.19 = (f32[2,2,16,1,128]{4,3,2,1,0:T(1,128)S(1)}, f32[2,2,16,1,128]{4,3,2,1,0:T(1,128)S(1)}, u32[]{:S(2)}, u32[]{:S(2)}) collective-permute-start(f32[2,2,16,1,128]{4,3,2,1,0:T(1,128)S(1)} %slice.724), channel_id=1, source_target_pairs={{0,1},{1,2},{2,3},{3,4},{4,5},{5,6},{6,7},{7,8},{8,9},{9,10},{10,1... | collective-permute-start | bytes 98312 | tf_op jit(solution)/shard_map/ppermute | solution.py:13
